TPU v7x, 256 devices: a whole 4x4x8 slice. The times are simulated.
256 devices in a mesh: tm: 32 (over y, x, core), space: 8 (over z).
Axes of the slice: x: 4, y: 4, z: 8, core: 2. Of those that a mesh axis runs over, the one named last changes fastest.
Arguments:
- latent_tokens: bfloat16 [64, 1792, 2240], P('tm', 'space'), may hold values from -6 to 6
- norm_gain: float32 [2240], replicated, may hold values from 0.5 to 1.5
- w_query: bfloat16 [2240, 1120], P('tm', 'space'), may hold values from -0.125 to 0.125
- w_key: bfloat16 [2240, 1120], P('tm', 'space'), may hold values from -0.125 to 0.125
- w_value: bfloat16 [2240, 1120], P('tm', 'space'), may hold values from -0.125 to 0.125
- out_gain: float32 [1120], replicated, may hold values from 0.5 to 1.5
- block_ids: int32 [64], P('tm'), may hold values from 0 to 15, never falling along the last dimension, each value on 1 to 8 neighbouring positions
Outputs:
- attended: bfloat16 [64, 1792, 1120], P('tm', 'space')
Inputs may be any that keep to these rules, and one draw needn't show every extreme that they name: `block_ids`: block numbers never fall from one frame to the next; each of the 16 blocks holds 1 to 8 frames and one holds exactly 8.
All inputs are finite; a program needn't handle non-finite values.
Results may differ from a plain program's by a relative error of at most 0.0065.
Values may be sent and summed in bfloat16 or wider, within the bound.
A program may use at most 192 MiB of HBM per device.

v0:
```python
import jax
import jax.numpy as jnp
from jax import lax
from jax.sharding import PartitionSpec as P

HEAD = 112
HEADS = 10


def gathered(weights):
    columns_full = lax.all_gather(jnp.stack(weights), "space", axis=2, tiled=True)
    return lax.all_gather(columns_full, "tm", axis=1, tiled=True)


def on_device(latent_tokens, norm_gain, w_query, w_key, w_value, out_gain, block_ids):
    frame_count, token_count, width = latent_tokens.shape
    row_count = frame_count * token_count
    values = latent_tokens.reshape(row_count, width).astype(jnp.float32)
    meansq = jnp.mean(values * values, axis=-1, keepdims=True)
    normed = (values * lax.rsqrt(meansq + 1e-06) * norm_gain).astype(jnp.bfloat16)
    pair = gathered((w_key, w_value))
    alone = gathered((w_query,))
    projected = jnp.einsum("rn,cnh->crh", normed, pair, preferred_element_type=jnp.float32)
    channels = projected.shape[2]
    headed = (frame_count, token_count, HEADS, HEAD)
    key = jax.nn.relu(projected[0]).astype(jnp.bfloat16).reshape(headed)
    value = projected[1].astype(jnp.bfloat16).reshape(headed)
    states = jnp.einsum("fthk,fthv->fhkv", key, value, preferred_element_type=jnp.float32)
    states = states.reshape(frame_count, channels, HEAD)
    mine = lax.psum_scatter(states, "space", scatter_dimension=1, tiled=True)
    everyone = lax.all_gather(mine.astype(jnp.bfloat16), "tm", tiled=True)
    all_ids = lax.all_gather(block_ids, "tm", tiled=True)
    reaches = (all_ids[None, :] <= block_ids[:, None]).astype(jnp.bfloat16)
    carried = jnp.einsum("fg,gkv->fkv", reaches, everyone, preferred_element_type=jnp.float32)
    carried = lax.all_gather(carried.astype(jnp.bfloat16), "space", axis=1, tiled=True)
    carried = carried.reshape(frame_count, HEADS, HEAD, HEAD)
    query = jnp.einsum("rn,cnh->crh", normed, alone, preferred_element_type=jnp.float32)[0]
    query = jax.nn.relu(query).astype(jnp.bfloat16).reshape(headed)
    numerator = jnp.einsum("fthk,fhkv->fthv", query, carried, preferred_element_type=jnp.float32)
    head_meansq = jnp.mean(numerator * numerator, axis=-1, keepdims=True)
    result = numerator * lax.rsqrt(head_meansq + 1e-06) * out_gain.reshape(HEADS, HEAD)
    return result.reshape(frame_count, token_count, channels).astype(jnp.bfloat16)


def solution(mesh):
    placed = (
        P("tm", "space", None),
        P(),
        P("tm", "space"),
        P("tm", "space"),
        P("tm", "space"),
        P(),
        P("tm"),
    )
    return jax.shard_map(
        on_device, mesh=mesh, in_specs=placed, out_specs=P("tm", "space", None), check_vma=False
    )
```

profile of v0, /device:TPU:6, one launch (start us, length us, event | category | flops | bytes accessed | tf_op | source)
XLA Modules:
  0.0 274.6 jit_solution(4759564278663120340)
XLA Ops:
  6.5 0.0 copy-start.3
  6.5 0.0 copy-start
  6.5 0.0 all-gather.8.cloned.1.call-start
  6.5 0.9 pad_maximum_fusion
  7.5 0.1 copy.40
  7.6 29.2 %all_gather.22 = bf16[2,70,1120]{1,0,2:T(2,128)(2,1)S(1)} all-gather(bf16[2,70,140]{1,0,2:T(2,128)(2,1)S(1)} %copy.40), channel_id=1, replica_groups=mesh['tm'=32,'space'=8] {'space'}, dimensions={2}, use_global_device_ids=true | all-gather | bytes 352800 | tf_op jit(solution)/shard_map/all_gather | solution.py:11
  36.9 2.2 copy.41
  39.0 0.0 copy-start.7
  39.0 0.0 copy-start.2
  39.0 0.0 all-gather.8.cloned.1.call-update
  39.1 0.0 all-gather.12.cloned.1.call-start
  39.1 0.0 copy-done.3
  39.1 0.1 copy.51
  39.2 25.1 %all-gather.2 = bf16[8,140,70]{2,1,0:T(8,128)(2,1)S(1)} all-gather(bf16[1,140,70]{2,1,0:T(8,128)(2,1)S(1)} %bitcast.50), channel_id=2, replica_groups=mesh['tm'=32,'space'=8] {'space'}, dimensions={0}, use_global_device_ids=true | all-gather | bytes 176400 | tf_op jit(solution)/shard_map/all_gather | solution.py:11
  64.3 0.1 reshape.90
  64.4 0.9 copy.65
  65.3 0.0 all-gather.12.cloned.1.call-update
  65.3 0.0 all-gather.10.cloned.1.call-start
  65.3 0.0 copy-done
  65.3 0.5 multiply_reduce_fusion
  65.8 0.1 rsqrt.21
  65.9 0.0 copy-done.7
  65.9 0.6 dynamic-slice.1
  67.1 0.0 copy-done.2
  67.1 1.8 fusion.3
  68.9 32.0 %all-gather.8.cloned.1.call-done = bf16[2,2240,1120]{2,0,1:T(2,128)(2,1)} async-done(((bf16[2,70,1120]{2,0,1:T(2,128)(2,1)}), bf16[2,2240,1120]{2,0,1:T(2,128)(2,1)}) %all-gather.8.cloned.1.call-update) | async-done | bytes 10035216 | tf_op jit(solution)/shard_map/all_gather | solution.py:12
  100.9 9.5 %fusion.4 = bf16[2,448,1120]{2,1,0:T(8,128)(2,1)S(1)} fusion(bf16[2,2240,1120]{2,0,1:T(2,128)(2,1)} %all-gather.8.cloned.1.call-done, bf16[448,2240]{1,0:T(8,128)(2,1)} %fusion.3), kind=kOutput, calls=%fused_computation.7 | convolution fusion | flops 4495769600 | bytes 14049280 | tf_op jit(solution)/shard_map/rn,cnh->crh/dot_general | solution.py:23
  110.4 1.2 fusion.14
  111.6 4.4 %reshape.88 = bf16[2,224,10,112]{3,2,1,0:T(8,128)(2,1)} reshape(bf16[1,448,1120]{2,1,0:T(8,128)(2,1)} %get-tuple-element.5) | data formatting | bytes 2007040 | tf_op jit(solution)/shard_map/convert_element_type | solution.py:26
  116.0 3.1 %reshape.89 = bf16[2,224,10,112]{3,2,1,0:T(8,128)(2,1)} reshape(bf16[1,448,1120]{2,1,0:T(8,128)(2,1)S(1)} %get-tuple-element.6) | data formatting | bytes 2007040 | tf_op jit(solution)/shard_map/convert_element_type | solution.py:27
  119.1 2.6 fusion.18
  121.8 0.0 copy-start.4
  121.8 0.0 copy-start.6
  121.8 0.0 copy-start.5
  121.8 4.2 %copy.47 = f32[2,1120,112]{2,0,1:T(2,128)S(1)} copy(f32[2,1120,112]{2,1,0:T(8,128)S(1)} %bitcast.46) | data formatting | bytes 2007040 | tf_op jit(solution)/shard_map/reshape | solution.py:29
  126.0 62.4 %all-reduce.3 = bf16[2,1120,112]{2,0,1:T(2,128)(2,1)} all-reduce(f32[2,1120,112]{2,0,1:T(2,128)S(1)} %copy.47), channel_id=4, replica_groups=mesh['tm'=32,'space'=8] {'space'}, use_global_device_ids=true, to_apply=%region_1.2.clone | all-reduce | flops 250880 | bytes 1505280
  188.4 0.9 dynamic-slice_convert_fusion
  189.3 0.6 copy.48
  190.0 0.0 all-gather.10.cloned.1.call-update
  190.0 0.0 copy-done.4
  190.0 0.1 mul.63
  190.1 0.0 copy-done.6
  190.1 0.6 dynamic-slice
  191.2 0.0 copy-done.5
  191.3 0.2 dynamic-update-slice
  191.5 14.1 %all-reduce = s32[64]{0:T(128)S(1)} all-reduce(s32[64]{0:T(128)S(1)} %dynamic-update-slice), channel_id=1, replica_groups=mesh['tm'=32,'space'=8] {'tm'}, use_global_device_ids=true, to_apply=%add | all-reduce | flops 64 | bytes 512
  205.6 1.9 multiply_convert_fusion
  207.5 0.0 copy-start.1
  207.5 0.0 all-gather.12.cloned.1.call-done
  207.5 8.1 %reshape.83 = bf16[2240,1120]{1,0:T(8,128)(2,1)} reshape(bf16[32,70,1120]{2,1,0:T(8,128)(2,1)} %all-gather.12.cloned.1.call-done) | data formatting | bytes 10035200
  215.6 0.0 copy-done.1
  215.6 5.3 %fusion.8 = bf16[1,448,1120]{2,1,0:T(8,128)(2,1)S(1)} fusion(bf16[448,2240]{1,0:T(8,128)(2,1)S(1)} %bitcast.48, bf16[2240,1120]{1,0:T(8,128)(2,1)} %reshape.83), kind=kOutput, calls=%fused_computation.10 | convolution fusion | flops 2248888320 | bytes 8028160 | tf_op jit(solution)/shard_map/rn,cnh->crh/dot_general | solution.py:37
  220.9 2.2 reshape.91
  223.1 13.1 %all-gather.10.cloned.1.call-done = bf16[64,140,112]{2,1,0:T(8,128)(2,1)} async-done(((bf16[2,140,112]{2,1,0:T(8,128)(2,1)}), bf16[64,140,112]{2,1,0:T(8,128)(2,1)}) %all-gather.10.cloned.1.call-update) | async-done | bytes 2007056 | tf_op jit(solution)/shard_map/all_gather | solution.py:31
  236.2 2.2 fusion.21
  238.4 27.0 %all_gather.25 = bf16[2,1120,112]{2,0,1:T(2,128)(2,1)S(1)} all-gather(bf16[2,140,112]{2,0,1:T(2,128)(2,1)S(1)} %fusion.21), channel_id=1, replica_groups=mesh['tm'=32,'space'=8] {'space'}, dimensions={1}, use_global_device_ids=true | all-gather | bytes 564480 | tf_op jit(solution)/shard_map/all_gather | solution.py:35
  265.4 0.9 fusion.9
  266.3 0.4 fusion.11
  266.7 1.4 copy.56
  (3 shorter events, 0.0 us)
Async XLA Ops:
  6.5 32.6 %copy-start.3 = (bf16[70,140]{1,0:T(8,128)(2,1)S(1)}, bf16[70,140]{1,0:T(8,128)(2,1)}, u32[]{:S(2)}) copy-start(bf16[70,140]{1,0:T(8,128)(2,1)} %param.9) | copy-start | bytes 58804
  6.5 58.8 %copy-start = (bf16[2,224,2240]{2,1,0:T(8,128)(2,1)S(1)}, bf16[2,224,2240]{2,1,0:T(8,128)(2,1)}, u32[]{:S(2)}) copy-start(bf16[2,224,2240]{2,1,0:T(8,128)(2,1)} %param.7) | copy-start | bytes 6021124
  6.5 94.4 %all-gather.8.cloned.1.call-start = ((), (), s32[]{:S(2)}) async-start(), calls=%async_computation | async-start | bytes 10644480 | tf_op jit(solution)/shard_map/all_gather | solution.py:12
  39.0 26.9 %copy-start.7 = (u32[256]{0:T(256)S(1)}, u32[256]{0:T(256)}, u32[]{:S(2)}) copy-start(u32[256]{0:T(256)} %constant.27) | copy-start | bytes 3076
  39.0 28.0 %copy-start.2 = (f32[2240]{0:T(1024)S(1)}, f32[2240]{0:T(1024)}, u32[]{:S(2)}) copy-start(f32[2240]{0:T(1024)} %param.8) | copy-start | bytes 26884
  39.1 168.4 %all-gather.12.cloned.1.call-start = ((), (), s32[]{:S(2)}) async-start(), calls=%async_computation.2 | async-start | bytes 5474304 | tf_op jit(solution)/shard_map/all_gather | solution.py:12
  65.3 170.9 %all-gather.10.cloned.1.call-start = ((), (), s32[]{:S(2)}) async-start(), calls=%async_computation.1 | async-start | bytes 2433024 | tf_op jit(solution)/shard_map/all_gather | solution.py:31
  121.8 68.2 %copy-start.4 = (f32[1120]{0:T(1024)S(1)}, f32[1120]{0:T(1024)}, u32[]{:S(2)}) copy-start(f32[1120]{0:T(1024)} %param.12) | copy-start | bytes 13444
  121.8 68.3 %copy-start.6 = (u32[256]{0:T(256)S(1)}, u32[256]{0:T(256)}, u32[]{:S(2)}) copy-start(u32[256]{0:T(256)} %constant.21) | copy-start | bytes 3076
  121.8 69.4 %copy-start.5 = (s32[2]{0:T(128)S(1)}, s32[2]{0:T(128)}, u32[]{:S(2)}) copy-start(s32[2]{0:T(128)} %param.13) | copy-start | bytes 28
  207.5 8.1 %copy-start.1 = (bf16[2,224,2240]{2,1,0:T(8,128)(2,1)S(1)}, bf16[2,224,2240]{2,1,0:T(8,128)(2,1)}, u32[]{:S(2)}) copy-start(bf16[2,224,2240]{2,1,0:T(8,128)(2,1)} %multiply_convert_fusion) | copy-start | bytes 6021124
Sparse Core Ops, SparseCore 0:
  39.2 61.6 all-gather.7
  103.5 51.7 all-gather.11
  190.1 46.0 all-gather.9
where the time goes:
time: 275 us
  blocking collectives  158 us (57%)
  waiting for transfers between devices  45.1 us (16%)
  local copies, waits for them, and re-layouts  29.9 us (11%)
  matrix products  20.5 us (7%)
  between operations  14.4 us (5%)
  other arithmetic  6.73 us (2%)
    unnamed x2, blocking collectives  76.5 us
    all_gather x2, blocking collectives, gathered(): lax.all_gather(jnp.stack(weights), 'space', axis=2, tiled=True)  54.3 us
    all_gather x2, waiting for transfers between devices, gathered(): return lax.all_gather(columns_full, 'tm', axis=1, tiled=True)  32 us
    all_gather x1, blocking collectives, on_device(): lax.all_gather(carried.astype(jnp.bfloat16), 'space', axis=1, tiled=True)  27 us
    all_gather x1, waiting for transfers between devices, on_device(): everyone = lax.all_gather(mine.astype(jnp.bfloat16), 'tm', tiled=True)  13.1 us
    unnamed x24, local copies, waits for them, and re-layouts  10.6 us
    dot_general x1, matrix products, on_device(): jnp.einsum('rn,cnh->crh', normed, pair, preferred_element_type=jnp.float32)  9.52 us
  transfers between devices with their start and end apart: 3, of which 2 were waited for; matrix products, arithmetic and copies ran while one was open for 18% of the time, Pallas kernels for 0%

commit v1 on v0

--- a/solution.py
+++ b/solution.py
@@ -9,7 +9,9 @@
 
 def gathered(weights):
     columns_full = lax.all_gather(jnp.stack(weights), "space", axis=2, tiled=True)
-    return lax.all_gather(columns_full, "tm", axis=1, tiled=True)
+    return jnp.concatenate(
+        lax.all_to_all(jnp.stack([columns_full] * lax.axis_size("tm")), "tm", 0, 0), axis=1
+    )
 
 
 def on_device(latent_tokens, norm_gain, w_query, w_key, w_value, out_gain, block_ids):

time: 275 us -> 362 us (1.32)
  waiting for transfers between devices: 45.1 us -> 108 us
  starting transfers between devices: 0.09 us -> 21.1 us
  local copies, waits for them, and re-layouts: 29.9 us -> 36 us
    all_to_all x0 -> x2, waiting for transfers between devices: none -> 93.2 us  [gathered(): lax.all_to_all(jnp.stack([columns_full] * lax.axis_size('tm')), 'tm', 0, 0)]
    all_gather x2 -> x0, waiting for transfers between devices: 32 us -> none  [gathered(): return lax.all_gather(columns_full, 'tm', axis=1, tiled=True)]
    all_to_all x0 -> x2, starting transfers between devices: none -> 21.1 us  [gathered(): lax.all_to_all(jnp.stack([columns_full] * lax.axis_size('tm')), 'tm', 0, 0)]
    another operation x0 -> x3, local copies, waits for them, and re-layouts: none -> 17.5 us  [the longest x2 9.41 us: gathered(): jnp.stack([columns_full] * lax.axis_size('tm'))]
    unnamed x24 -> x25, local copies, waits for them, and re-layouts: 10.6 us -> 1.89 us
  transfers between devices with their start and end apart: 3 -> 3, of which waited for: 2 -> 2; matrix products, arithmetic and copies ran while one was open for 18% -> 12% of each run, Pallas kernels for 0% -> 0%
where the time goes in v1:
time: 362 us; the launch traced here: 361 us
  blocking collectives  157 us (43%)
  waiting for transfers between devices  108 us (30%)
  local copies, waits for them, and re-layouts  36 us (10%)
  starting transfers between devices  21.1 us (6%)
  matrix products  19.6 us (5%)
  between operations  14.9 us (4%)
  other arithmetic  4.68 us (1%)
    all_to_all x2, waiting for transfers between devices, gathered(): lax.all_to_all(jnp.stack([columns_full] * lax.axis_size('tm')), 'tm', 0, 0)  93.2 us
    unnamed x2, blocking collectives  75.6 us
    all_gather x2, blocking collectives, gathered(): lax.all_gather(jnp.stack(weights), 'space', axis=2, tiled=True)  54.2 us
    all_gather x1, blocking collectives, on_device(): lax.all_gather(carried.astype(jnp.bfloat16), 'space', axis=1, tiled=True)  27 us
    all_to_all x2, starting transfers between devices, gathered(): lax.all_to_all(jnp.stack([columns_full] * lax.axis_size('tm')), 'tm', 0, 0)  21.1 us
    all_gather x1, waiting for transfers between devices, on_device(): everyone = lax.all_gather(mine.astype(jnp.bfloat16), 'tm', tiled=True)  14.7 us
    another operation x2, local copies, waits for them, and re-layouts, gathered(): jnp.stack([columns_full] * lax.axis_size('tm'))  9.41 us
    dot_general x1, matrix products, on_device(): jnp.einsum('rn,cnh->crh', normed, pair, preferred_element_type=jnp.float32)  9.13 us
  transfers between devices with their start and end apart: 3, of which 2 were waited for; matrix products, arithmetic and copies ran while one was open for 12% of the time, Pallas kernels for 0%

profile of v1, /device:TPU:6, one launch (start us, length us, event | category | flops | bytes accessed | tf_op | source)
XLA Modules:
  0.0 361.0 jit_solution(17863082734008274876)
XLA Ops:
  6.5 0.8 pad_maximum_fusion
  7.3 0.1 copy.41
  7.5 29.2 %all_gather.18 = bf16[2,70,1120]{1,0,2:T(2,128)(2,1)S(1)} all-gather(bf16[2,70,140]{1,0,2:T(2,128)(2,1)S(1)} %copy.41), channel_id=1, replica_groups=mesh['tm'=32,'space'=8] {'space'}, dimensions={2}, use_global_device_ids=true | all-gather | bytes 352800 | tf_op jit(solution)/shard_map/all_gather | solution.py:11
  36.7 1.4 copy.42
  38.1 6.8 %stack.15 = bf16[32,2,70,1120]{3,1,2,0:T(2,128)(2,1)} broadcast(bf16[2,70,1120]{2,0,1:T(2,128)(2,1)S(1)} %copy.42), dimensions={1,2,3} | broadcast | bytes 10348800 | tf_op jit(solution)/shard_map/stack | solution.py:13
  44.8 0.0 copy-start.3
  44.9 0.0 copy-start.8
  44.9 0.0 copy-start
  44.9 7.8 %all-to-all-start = ((bf16[32,2,70,1120]{3,1,2,0:T(2,128)(2,1)}), bf16[32,2,70,1120]{3,1,2,0:T(2,128)(2,1)}, u32[]{:S(2)}, u32[]{:S(2)}) async-start(bf16[32,2,70,1120]{3,1,2,0:T(2,128)(2,1)} %stack.15), calls=%async_computation | async-start | bytes 20643840 | tf_op jit(solution)/shard_map/all_to_all | solution.py:13
  52.6 0.0 copy-start.4
  52.6 0.0 copy-done.3
  52.6 0.1 copy.52
  52.8 25.0 %all-gather.1 = bf16[8,140,70]{2,1,0:T(8,128)(2,1)S(1)} all-gather(bf16[1,140,70]{2,1,0:T(8,128)(2,1)S(1)} %bitcast.46), channel_id=2, replica_groups=mesh['tm'=32,'space'=8] {'space'}, dimensions={0}, use_global_device_ids=true | all-gather | bytes 176400 | tf_op jit(solution)/shard_map/all_gather | solution.py:11
  77.8 0.1 reshape.104
  77.9 0.2 copy.67
  78.1 0.0 copy-done.8
  78.1 0.6 dynamic-slice.1
  79.3 0.0 copy-done
  79.3 0.5 fusion.2
  79.8 0.0 copy-done.4
  79.8 1.8 fusion.4
  81.7 93.2 %all-to-all-done = bf16[32,2,70,1120]{3,1,2,0:T(2,128)(2,1)} async-done(((bf16[32,2,70,1120]{3,1,2,0:T(2,128)(2,1)}), bf16[32,2,70,1120]{3,1,2,0:T(2,128)(2,1)}, u32[]{:S(2)}, u32[]{:S(2)}) %all-to-all-start) | async-done | bytes 10035232 | tf_op jit(solution)/shard_map/all_to_all | solution.py:13
  174.9 2.6 stack.17
  177.6 0.0 copy-start.1
  177.6 13.3 %all-to-all-start.1 = ((bf16[32,1,70,1120]{3,2,1,0:T(8,128)(2,1)}), bf16[32,1,70,1120]{3,2,1,0:T(8,128)(2,1)}, u32[]{:S(2)}, u32[]{:S(2)}) async-start(bf16[32,1,70,1120]{3,2,1,0:T(8,128)(2,1)} %stack.17), calls=%async_computation.1 | async-start | bytes 10616832 | tf_op jit(solution)/shard_map/all_to_all | solution.py:13
  190.9 0.0 all-gather.4.cloned.1.call-start
  190.9 0.0 copy-done.1
  190.9 9.1 %fusion.5 = bf16[2,448,1120]{2,1,0:T(8,128)(2,1)S(1)} fusion(bf16[448,2240,1]{1,0,2:T(8,128)(2,1)S(1)} %bitcast.43, bf16[2,2240,1120]{2,0,1:T(2,128)(2,1)} %bitcast.5), kind=kOutput, calls=%fused_computation.7 | convolution fusion | flops 4495769600 | bytes 14049280 | tf_op jit(solution)/shard_map/rn,cnh->crh/dot_general | solution.py:25
  200.1 1.2 fusion.15
  201.2 3.4 reshape.102
  204.7 3.1 reshape.103
  207.8 2.1 fusion.18
  209.9 0.0 copy-start.5
  209.9 0.0 copy-start.7
  209.9 0.0 copy-start.6
  209.9 4.2 %copy.48 = f32[2,1120,112]{2,0,1:T(2,128)S(1)} copy(f32[2,1120,112]{2,1,0:T(8,128)S(1)} %bitcast.41) | data formatting | bytes 2007040 | tf_op jit(solution)/shard_map/reshape | solution.py:31
  214.1 60.8 %all-reduce.3 = bf16[2,1120,112]{2,0,1:T(2,128)(2,1)S(1)} all-reduce(f32[2,1120,112]{2,0,1:T(2,128)S(1)} %copy.48), channel_id=3, replica_groups=mesh['tm'=32,'space'=8] {'space'}, use_global_device_ids=true, to_apply=%region_1.2.clone | all-reduce | flops 250880 | bytes 1505280
  274.9 0.1 dynamic-slice_convert_fusion
  274.9 0.6 copy.49
  275.6 0.0 all-gather.4.cloned.1.call-update
  275.6 0.0 copy-done.5
  275.6 0.1 mul.53
  275.7 0.0 copy-done.7
  275.7 0.6 dynamic-slice
  277.0 0.0 copy-done.6
  277.0 0.2 dynamic-update-slice
  277.2 14.8 %all-reduce = s32[64]{0:T(128)S(1)} all-reduce(s32[64]{0:T(128)S(1)} %dynamic-update-slice), channel_id=1, replica_groups=mesh['tm'=32,'space'=8] {'tm'}, use_global_device_ids=true, to_apply=%add | all-reduce | flops 64 | bytes 512
  292.0 0.0 copy-start.2
  292.0 0.0 all-to-all-done.1
  292.0 8.1 %reshape.90 = bf16[2240,1120]{1,0:T(8,128)(2,1)} reshape(bf16[32,1,70,1120]{3,2,1,0:T(8,128)(2,1)} %all-to-all-done.1) | data formatting | bytes 10035200 | tf_op jit(solution)/shard_map/reshape.2
  300.1 0.0 copy-done.2
  300.2 5.3 %fusion.9 = bf16[1,448,1120]{2,1,0:T(8,128)(2,1)S(1)} fusion(bf16[448,2240]{1,0:T(8,128)(2,1)S(1)} %bitcast.44, bf16[2240,1120]{1,0:T(8,128)(2,1)} %reshape.90), kind=kOutput, calls=%fused_computation.10 | convolution fusion | flops 2248888320 | bytes 8028160 | tf_op jit(solution)/shard_map/rn,cnh->crh/dot_general | solution.py:39
  305.4 2.2 reshape.105
  307.6 14.7 %all-gather.4.cloned.1.call-done = bf16[64,140,112]{2,1,0:T(8,128)(2,1)} async-done(((bf16[2,140,112]{2,1,0:T(8,128)(2,1)}), bf16[64,140,112]{2,1,0:T(8,128)(2,1)}) %all-gather.4.cloned.1.call-update) | async-done | bytes 2007056 | tf_op jit(solution)/shard_map/all_gather | solution.py:33
  322.3 2.2 fusion.21
  324.5 27.0 %all_gather.20 = bf16[2,1120,112]{2,0,1:T(2,128)(2,1)S(1)} all-gather(bf16[2,140,112]{2,0,1:T(2,128)(2,1)S(1)} %fusion.21), channel_id=1, replica_groups=mesh['tm'=32,'space'=8] {'space'}, dimensions={1}, use_global_device_ids=true | all-gather | bytes 564480 | tf_op jit(solution)/shard_map/all_gather | solution.py:37
  351.5 0.9 fusion.10
  352.5 0.4 fusion.12
  352.8 1.4 copy.57
  (3 shorter events, 0.0 us)
Async XLA Ops:
  44.8 7.8 %copy-start.3 = (bf16[70,140]{1,0:T(8,128)(2,1)S(1)}, bf16[70,140]{1,0:T(8,128)(2,1)}, u32[]{:S(2)}) copy-start(bf16[70,140]{1,0:T(8,128)(2,1)} %param.9) | copy-start | bytes 58804
  44.9 33.2 %copy-start.8 = (u32[256]{0:T(256)S(1)}, u32[256]{0:T(256)}, u32[]{:S(2)}) copy-start(u32[256]{0:T(256)} %constant.27) | copy-start | bytes 3076
  44.9 34.5 %copy-start = (bf16[2,224,2240]{2,1,0:T(8,128)(2,1)S(1)}, bf16[2,224,2240]{2,1,0:T(8,128)(2,1)}, u32[]{:S(2)}) copy-start(bf16[2,224,2240]{2,1,0:T(8,128)(2,1)} %param.7) | copy-start | bytes 6021124
  44.9 130.1 %all-to-all-start = ((bf16[32,2,70,1120]{3,1,2,0:T(2,128)(2,1)}), bf16[32,2,70,1120]{3,1,2,0:T(2,128)(2,1)}, u32[]{:S(2)}, u32[]{:S(2)}) async-start(bf16[32,2,70,1120]{3,1,2,0:T(2,128)(2,1)} %stack.15), calls=%async_computation | async-start | bytes 20643840 | tf_op jit(solution)/shard_map/all_to_all | solution.py:13
  52.6 27.2 %copy-start.4 = (f32[2240]{0:T(1024)S(1)}, f32[2240]{0:T(1024)}, u32[]{:S(2)}) copy-start(f32[2240]{0:T(1024)} %param.8) | copy-start | bytes 26884
  177.6 13.4 %copy-start.1 = (bf16[2,224,2240]{2,1,0:T(8,128)(2,1)S(1)}, bf16[2,224,2240]{2,1,0:T(8,128)(2,1)}, u32[]{:S(2)}) copy-start(bf16[2,224,2240]{2,1,0:T(8,128)(2,1)} %fusion.4) | copy-start | bytes 6021124
  177.6 114.4 %all-to-all-start.1 = ((bf16[32,1,70,1120]{3,2,1,0:T(8,128)(2,1)}), bf16[32,1,70,1120]{3,2,1,0:T(8,128)(2,1)}, u32[]{:S(2)}, u32[]{:S(2)}) async-start(bf16[32,1,70,1120]{3,2,1,0:T(8,128)(2,1)} %stack.17), calls=%async_computation.1 | async-start | bytes 10616832 | tf_op jit(solution)/shard_map/all_to_all | solution.py:13
  190.9 131.5 %all-gather.4.cloned.1.call-start = ((), (), s32[]{:S(2)}) async-start(), calls=%async_computation.2 | async-start | bytes 2433024 | tf_op jit(solution)/shard_map/all_gather | solution.py:33
  209.9 65.7 %copy-start.5 = (f32[1120]{0:T(1024)S(1)}, f32[1120]{0:T(1024)}, u32[]{:S(2)}) copy-start(f32[1120]{0:T(1024)} %param.12) | copy-start | bytes 13444
  209.9 65.8 %copy-start.7 = (u32[256]{0:T(256)S(1)}, u32[256]{0:T(256)}, u32[]{:S(2)}) copy-start(u32[256]{0:T(256)} %constant.21) | copy-start | bytes 3076
  209.9 67.1 %copy-start.6 = (s32[2]{0:T(128)S(1)}, s32[2]{0:T(128)}, u32[]{:S(2)}) copy-start(s32[2]{0:T(128)} %param.13) | copy-start | bytes 28
  292.0 8.1 %copy-start.2 = (bf16[2,224,2240]{2,1,0:T(8,128)(2,1)S(1)}, bf16[2,224,2240]{2,1,0:T(8,128)(2,1)}, u32[]{:S(2)}) copy-start(bf16[2,224,2240]{2,1,0:T(8,128)(2,1)} %fusion.4) | copy-start | bytes 6021124
Sparse Core Ops, SparseCore 0:
  275.7 46.5 all-gather.3
